TPU v7x, 512 devices: a whole 4x4x16 slice. The times are simulated.
512 devices in a mesh: tile: 64 (over x, z_lo, core), agent: 8 (over z_hi, y).
Axes of the slice: x: 4, y: 4, z: 16 (z_hi: 2, z_lo: 8; z = z_hi * 8 + z_lo), core: 2. Of those that a mesh axis runs over, the one named last changes fastest.
Arguments:
- states: float32 [8, 8, 128, 256], P('agent', None, 'tile'), may hold values from -6 to 6
- footprints: float32 [64, 64, 64, 512], P('agent', 'tile'), may hold values from -0.25 to 0.25
- offsets: int32 [64, 64], P('agent', 'tile'), may hold values from 0 to 1984, as said below
- measured: float32 [64, 8, 2048], P('agent', None, 'tile'), may hold values from -9 to 9
- weights: float32 [64, 8, 2048], P('agent', None, 'tile'), may hold values from 0.2 to 5
Outputs:
- new_states: float32 [8, 8, 128, 256], P('agent', None, 'tile')
- prior_volume: float32 [8, 128, 256], P(None, 'tile')
Inputs may be any that keep to these rules, and one draw needn't show every extreme that they name: For one agent and one tile t, the values offsets[v, t] // 32 differ between the agent's 8 views v.
All inputs are finite; a program needn't handle non-finite values.
Results may differ from a plain program's by a relative error of at most 0.0003.
Values sent between devices are 32-bit elements; how exact they have to be, the bound alone decides.
No kernel may reach another device: no remote copies, remote signals or barrier semaphores. Data moves between devices by JAX's collectives and lax.ppermute only.
A program may use at most 64 MiB of HBM per device.

v0:
```python
import jax
import jax.numpy as jnp
from jax import lax
from jax.sharding import PartitionSpec as P

SWEEPS = 2
STEP_SIZE = 0.25
RELAX = 0.6
QRATIO = 0.6


def with_halo(value, sides, width):
    for axis, dim in sides:
        count, length = (lax.axis_size(axis), value.shape[dim])
        up = [(i, (i + 1) % count) for i in range(count - 1)]
        down = [(j, i) for i, j in up]
        last = lax.slice_in_dim(value, length - width, length, axis=dim)
        first = lax.slice_in_dim(value, 0, width, axis=dim)
        before = lax.ppermute(last, axis, up)
        after = lax.ppermute(first, axis, down)
        value = jnp.concatenate([before, value, after], axis=dim)
    return value


def neighbour_table():
    offsets_nb = []
    for a in (-1, 0, 1):
        for b in (-1, 0, 1):
            for c in (-1, 0, 1):
                if a != 0 or b != 0 or c != 0:
                    offsets_nb.append((a, b, c, 1.0 / (a * a + b * b + c * c) ** 0.5))
    total = sum((item[3] for item in offsets_nb))
    return [(a, b, c, 4.0 * w / total) for a, b, c, w in offsets_nb]


def sweep_update(padded, average):
    depth, height, width = average.shape
    centre = padded[1 : 1 + depth, 1 : 1 + height, 1 : 1 + width]
    numerator = average
    denominator = jnp.ones_like(average)
    for a, b, c, weight_nb in neighbour_table():
        neighbour = padded[1 + a : 1 + a + depth, 1 + b : 1 + b + height, 1 + c : 1 + c + width]
        differ = centre - neighbour
        powered = jnp.power(differ * differ, 0.4)
        coefficient = weight_nb * (1.0 + QRATIO * powered) / ((1.0 + powered) * (1.0 + powered))
        numerator = numerator + coefficient * neighbour
        denominator = denominator + coefficient
    return numerator / denominator


def shards(states, footprints, offsets, measured, weights):
    current = states[0]
    blocks = footprints[:, 0]
    offsets_dev = offsets[:, 0]
    slices, height, width = current.shape
    views, foot, pixels = blocks.shape
    share = measured.shape[2]
    n_tile = lax.axis_size("tile")
    detector = share * n_tile
    n_agent = lax.axis_size("agent")
    zero_index = jnp.int32(0)
    volume = current.reshape(slices, pixels)
    projected = jnp.einsum("sp,vbp->vsb", volume, blocks, precision=lax.Precision.HIGHEST)
    partial_value = jnp.stack(
        [
            lax.dynamic_update_slice(
                jnp.zeros((slices, detector), jnp.float32),
                projected[view],
                (zero_index, offsets_dev[view]),
            )
            for view in range(views)
        ]
    )
    share_sum = lax.psum_scatter(partial_value, "tile", scatter_dimension=2, tiled=True)
    residual_share = weights * (share_sum - measured)
    residual = lax.all_gather(residual_share, "tile", axis=2, tiled=True)
    windows = jnp.stack(
        [
            lax.dynamic_slice(residual[view], (zero_index, offsets_dev[view]), (slices, foot))
            for view in range(views)
        ]
    )
    gradient = jnp.einsum("vsb,vbp->sp", windows, blocks, precision=lax.Precision.HIGHEST)
    fitted = current - STEP_SIZE * gradient.reshape(slices, height, width)
    reflect = 2.0 * fitted - current
    brick_mean = lax.psum_scatter(reflect, "agent", scatter_dimension=0, tiled=True) / n_agent
    smoothed = brick_mean
    for sweep_index in range(SWEEPS):
        padded = with_halo(smoothed, (("tile", 1), ("agent", 0)), 1)
        padded = jnp.pad(padded, ((0, 0), (0, 0), (1, 1)))
        smoothed = sweep_update(padded, brick_mean)
    prior_vol = lax.all_gather(smoothed, "agent", axis=0, tiled=True)
    current = (1.0 - RELAX) * current + RELAX * (2.0 * prior_vol - reflect)
    return (current[None], prior_vol)


def solution(mesh):
    in_specs = (
        P("agent", None, "tile", None),
        P("agent", "tile", None, None),
        P("agent", "tile"),
        P("agent", None, "tile"),
        P("agent", None, "tile"),
    )
    out_specs = (P("agent", None, "tile", None), P(None, "tile", None))
    return jax.shard_map(shards, mesh=mesh, in_specs=in_specs, out_specs=out_specs, check_vma=False)
```

profile of v0, /device:TPU:24, one launch (start us, length us, event | category | flops | bytes accessed | tf_op | source)
XLA Modules:
  0.0 878.3 jit_solution(8798802146423708650)
XLA Ops:
  7.2 1.6 fusion.17
  19.1 0.7 reshape.62
  19.8 2.6 convolution_bitcast_fusion
  23.0 0.3 dynamic_update_slice.32
  24.0 0.3 dynamic_update_slice.33
  24.9 0.3 dynamic_update_slice.34
  25.9 0.3 dynamic_update_slice.35
  27.0 0.3 dynamic_update_slice.36
  28.0 0.3 dynamic_update_slice.37
  28.9 0.3 dynamic_update_slice.38
  29.9 0.3 dynamic_update_slice.39
  30.2 4.6 copy.26
  34.8 6.5 reshape.66
  41.3 1.3 dynamic-slice.8
  42.6 444.4 %reduce-scatter.4.cloned.1.call-done = f32[32,64]{1,0:T(8,128)} async-done(((f32[2048,64]{1,0:T(8,128)}), f32[32,64]{1,0:T(8,128)}) %reduce-scatter.4.cloned.1.call-update) | async-done | bytes 8208
  487.0 0.8 reshape.67
  487.8 0.1 copy.27
  487.9 0.1 copy.12
  488.0 166.6 %all_gather.6 = f32[8,8,2048]{1,0,2:T(8,128)} all-gather(f32[8,8,32]{1,0,2:T(8,128)S(1)} %copy.12), channel_id=1, replica_groups=mesh['tile'=64,'agent'=8] {'tile'}, dimensions={2}, use_global_device_ids=true | all-gather | bytes 532480 | tf_op jit(solution)/shard_map/all_gather | solution.py:76
  654.7 29.4 %fusion.13 = (f32[1,8,2048]{1,0,2:T(1,128)}, f32[1,8,2048]{1,0,2:T(1,128)}, f32[1,8,2048]{1,0,2:T(1,128)}, f32[1,8,2048]{1,0,2:T(1,128)}, f32[1,8,2048]{1,0,2:T(...) fusion(f32[8,8,2048]{1,0,2:T(8,128)} %all_gather.6), kind=kLoop, calls=%fused_computation.61 | loop fusion | bytes 1048576 | tf_op jit(solution)/shard_map/slice | solution.py:79
  684.1 0.8 constant_dynamic-slice_fusion
  684.8 0.1 copy.41
  684.9 0.8 constant_dynamic-slice_fusion.2
  685.7 0.1 copy.37
  685.8 0.8 constant_dynamic-slice_fusion.4
  686.6 0.1 copy.29
  687.0 0.6 fusion.3
  687.7 65.1 %all-reduce.2 = f32[8,2,256]{2,1,0:T(2,128)S(1)} all-reduce(f32[8,2,256]{2,1,0:T(2,128)S(1)} %copy.22), channel_id=3, replica_groups=mesh['tile'=64,'agent'=8] {'agent'}, use_global_device_ids=true, to_apply=%region_1.0.clone | all-reduce | flops 4096 | bytes 32768
  752.8 0.7 dynamic-slice_multiply_fusion
  753.5 1.3 collective-permute-start
  754.8 1.3 collective-permute-start.1
  756.1 1.7 collective-permute-done.1
  757.8 15.0 %collective-permute-start.2 = (f32[1,4,256]{2,1,0:T(4,128)S(1)}, f32[1,4,256]{2,1,0:T(4,128)S(1)}, u32[]{:S(2)}, u32[]{:S(2)}) collective-permute-start(f32[1,4,256]{2,1,0:T(4,128)S(1)} %pad_maximum_fusion), channel_id=1, source_target_pairs={{0,1},{1,2},{2,3},{3,4},{4,5},{5,6},{6,7},{8,9},{9,10},{10,11},{11... | collective-permute-start | bytes 12296 | tf_op jit(solution)/shard_map/ppermute | solution.py:19
  772.8 1.9 collective-permute-start.3
  774.8 14.4 %collective-permute-done.3 = f32[1,4,256]{2,1,0:T(4,128)S(1)} collective-permute-done((f32[1,4,256]{2,1,0:T(4,128)S(1)}, f32[1,4,256]{2,1,0:T(4,128)S(1)}, u32[]{:S(2)}, u32[]{:S(2)}) %collective-permute-start.3) | collective-permute-done | bytes 4128 | tf_op jit(solution)/shard_map/ppermute | solution.py:20
  789.2 0.1 select_maximum_fusion.4
  789.3 0.2 add_divide_fusion.1
  789.5 1.3 collective-permute-start.4
  790.8 1.3 collective-permute-start.5
  792.1 1.7 collective-permute-done.5
  793.9 1.9 collective-permute-start.6
  795.8 3.9 collective-permute-start.7
  799.7 12.4 %collective-permute-done.7 = f32[1,4,256]{2,1,0:T(4,128)S(1)} collective-permute-done((f32[1,4,256]{2,1,0:T(4,128)S(1)}, f32[1,4,256]{2,1,0:T(4,128)S(1)}, u32[]{:S(2)}, u32[]{:S(2)}) %collective-permute-start.7) | collective-permute-done | bytes 4128 | tf_op jit(solution)/shard_map/ppermute | solution.py:20
  812.1 0.1 select_maximum_fusion
  812.2 0.9 add_divide_fusion
  813.1 57.1 %all_gather.7 = f32[8,2,256]{2,1,0:T(2,128)S(1)} all-gather(f32[1,2,256]{2,1,0:T(2,128)S(1)} %add_divide_fusion), channel_id=1, replica_groups=mesh['tile'=64,'agent'=8] {'agent'}, dimensions={0}, use_global_device_ids=true | all-gather | bytes 18432 | tf_op jit(solution)/shard_map/all_gather | solution.py:92
  870.2 0.6 copy.24
  870.8 0.6 copy.81
  (52 shorter events, 0.6 us)
Async XLA Ops:
  7.2 479.8 %reduce-scatter.4.cloned.1.call-start = ((), (), s32[]{:S(2)}) async-start(), calls=%async_computation.1 | async-start | bytes 1064960
  30.2 457.7 %copy-start.2 = (f32[8,8,32]{2,1,0:T(8,128)S(1)}, f32[8,8,32]{2,1,0:T(8,128)}, u32[]{:S(2)}) copy-start(f32[8,8,32]{2,1,0:T(8,128)} %param.9) | copy-start | bytes 24580
  30.2 457.7 %copy-start.3 = (f32[8,8,32]{2,1,0:T(8,128)S(1)}, f32[8,8,32]{2,1,0:T(8,128)}, u32[]{:S(2)}) copy-start(f32[8,8,32]{2,1,0:T(8,128)} %param.8) | copy-start | bytes 24580
  654.7 32.4 %copy-start = (f32[8,1,64,512]{3,2,1,0:T(8,128)S(1)}, f32[8,1,64,512]{3,2,1,0:T(8,128)}, u32[]{:S(2)}) copy-start(f32[8,1,64,512]{3,2,1,0:T(8,128)} %param.6) | copy-start | bytes 3145732
  654.7 32.4 %copy-start.1 = (f32[1,8,2,256]{3,2,1,0:T(2,128)S(1)}, f32[1,8,2,256]{3,2,1,0:T(2,128)}, u32[]{:S(2)}) copy-start(f32[1,8,2,256]{3,2,1,0:T(2,128)} %param.5) | copy-start | bytes 49156
  753.5 2.6 collective-permute-start
  754.8 3.1 collective-permute-start.1
  757.8 16.9 %collective-permute-start.2 = (f32[1,4,256]{2,1,0:T(4,128)S(1)}, f32[1,4,256]{2,1,0:T(4,128)S(1)}, u32[]{:S(2)}, u32[]{:S(2)}) collective-permute-start(f32[1,4,256]{2,1,0:T(4,128)S(1)} %pad_maximum_fusion), channel_id=1, source_target_pairs={{0,1},{1,2},{2,3},{3,4},{4,5},{5,6},{6,7},{8,9},{9,10},{10,11},{11... | collective-permute-start | bytes 12296 | tf_op jit(solution)/shard_map/ppermute | solution.py:19
  772.8 16.3 %collective-permute-start.3 = (f32[1,4,256]{2,1,0:T(4,128)S(1)}, f32[1,4,256]{2,1,0:T(4,128)S(1)}, u32[]{:S(2)}, u32[]{:S(2)}) collective-permute-start(f32[1,4,256]{2,1,0:T(4,128)S(1)} %pad_maximum_fusion), channel_id=1, source_target_pairs={{1,0},{2,1},{3,2},{4,3},{5,4},{6,5},{7,6},{9,8},{10,9},{11,10},{12... | collective-permute-start | bytes 12296 | tf_op jit(solution)/shard_map/ppermute | solution.py:20
  789.5 2.6 collective-permute-start.4
  790.8 3.1 collective-permute-start.5
  793.9 5.9 collective-permute-start.6
  795.8 16.3 %collective-permute-start.7 = (f32[1,4,256]{2,1,0:T(4,128)S(1)}, f32[1,4,256]{2,1,0:T(4,128)S(1)}, u32[]{:S(2)}, u32[]{:S(2)}) collective-permute-start(f32[1,4,256]{2,1,0:T(4,128)S(1)} %pad_maximum_fusion.1), channel_id=1, source_target_pairs={{1,0},{2,1},{3,2},{4,3},{5,4},{6,5},{7,6},{9,8},{10,9},{11,10},{12... | collective-permute-start | bytes 12296 | tf_op jit(solution)/shard_map/ppermute | solution.py:20
Sparse Core Ops, SparseCore 0:
  41.4 445.4 reduce-scatter.3
where the time goes:
time: 879 us; the launch traced here: 878 us
  waiting for transfers between devices  475 us (54%)
  blocking collectives  289 us (33%)
  local copies, waits for them, and re-layouts  51.8 us (6%)
  between operations  29.8 us (3%)
  starting transfers between devices  28 us (3%)
    unnamed x2, waiting for transfers between devices  444 us
    all_gather x1, blocking collectives, shards(): residual = lax.all_gather(residual_share, 'tile', axis=2, tiled=True)  167 us
    unnamed x1, blocking collectives  65.1 us
    all_gather x1, blocking collectives, shards(): prior_vol = lax.all_gather(smoothed, 'agent', axis=0, tiled=True)  57.1 us
    ppermute x4, waiting for transfers between devices, with_halo(): after = lax.ppermute(first, axis, down)  30.3 us
    slice x1, local copies, waits for them, and re-layouts, shards(): residual[view]  29.4 us
    ppermute x4, starting transfers between devices, with_halo(): before = lax.ppermute(last, axis, up)  19.5 us
  transfers between devices with their start and end apart: 9, of which 5 were waited for; matrix products, arithmetic and copies ran while one was open for 0% of the time, Pallas kernels for 0%

commit v1 on v0

--- a/solution.py
+++ b/solution.py
@@ -73,7 +73,12 @@
     )
     share_sum = lax.psum_scatter(partial_value, "tile", scatter_dimension=2, tiled=True)
     residual_share = weights * (share_sum - measured)
-    residual = lax.all_gather(residual_share, "tile", axis=2, tiled=True)
+    residual = jnp.concatenate(
+        jax.lax.all_to_all(
+            jnp.stack([residual_share] * jax.lax.psum(1, "tile"), axis=0), "tile", 0, 0
+        ),
+        2,
+    )
     windows = jnp.stack(
         [
             lax.dynamic_slice(residual[view], (zero_index, offsets_dev[view]), (slices, foot))

time: 879 us -> 743 us (0.85)
  the two profiles are of different devices: /device:TPU:24 before, /device:TPU:30 now
where the time goes in v1:
time: 743 us; the launch traced here: 742 us
  waiting for transfers between devices  462 us (62%)
  blocking collectives  122 us (16%)
  starting transfers between devices  93.3 us (13%)
  between operations  29.4 us (4%)
  local copies, waits for them, and re-layouts  27.5 us (4%)
    unnamed x2, waiting for transfers between devices  406 us
    unnamed x1, blocking collectives  65.2 us
    all_gather x1, blocking collectives, shards(): prior_vol = lax.all_gather(smoothed, 'agent', axis=0, tiled=True)  57.1 us
    all_to_all x1, starting transfers between devices, shards(): jax.lax.all_to_all(jnp.stack([residual_share] * jax.lax.psum(1, 'tile'),...  44.4 us
    ppermute x4, waiting for transfers between devices, with_halo(): after = lax.ppermute(first, axis, down)  29.3 us
    ppermute x4, starting transfers between devices, with_halo(): after = lax.ppermute(first, axis, down)  28.1 us
    all_to_all x1, waiting for transfers between devices, shards(): jax.lax.all_to_all(jnp.stack([residual_share] * jax.lax.psum(1, 'tile'),...  27.2 us
    ppermute x4, starting transfers between devices, with_halo(): before = lax.ppermute(last, axis, up)  20.7 us
  transfers between devices with their start and end apart: 10, of which 6 were waited for; matrix products, arithmetic and copies ran while one was open for 0% of the time, Pallas kernels for 0%

profile of v1, /device:TPU:30, one launch (start us, length us, event | category | flops | bytes accessed | tf_op | source)
XLA Modules:
  0.0 741.9 jit_solution(16554041671375853828)
XLA Ops:
  7.2 1.6 fusion.17
  18.8 0.7 reshape.69
  19.5 2.6 convolution_bitcast_fusion
  22.7 0.3 dynamic_update_slice.32
  23.7 0.3 dynamic_update_slice.33
  24.6 0.3 dynamic_update_slice.34
  25.6 0.3 dynamic_update_slice.35
  26.5 0.3 dynamic_update_slice.36
  27.5 0.3 dynamic_update_slice.37
  28.5 0.3 dynamic_update_slice.38
  29.5 0.3 dynamic_update_slice.39
  29.8 4.6 copy.29
  34.4 6.5 reshape.73
  40.9 405.9 %reduce-scatter.4.cloned.1.call-done = f32[32,64]{1,0:T(8,128)} async-done(((f32[2048,64]{1,0:T(8,128)}), f32[32,64]{1,0:T(8,128)}) %reduce-scatter.4.cloned.1.call-update) | async-done | bytes 8208
  446.7 0.8 reshape.74
  447.7 0.2 stack.26
  447.9 1.7 reshape.76
  449.6 44.4 %all-to-all-start = ((f32[64,1,2048]{2,1,0:T(1,128)}), f32[64,1,2048]{2,1,0:T(1,128)S(1)}, u32[]{:S(2)}, u32[]{:S(2)}) async-start(f32[64,1,2048]{2,1,0:T(1,128)} %reshape.76), calls=%async_computation | async-start | bytes 1048576 | tf_op jit(solution)/shard_map/all_to_all | solution.py:77
  494.0 1.3 dynamic-slice
  495.3 27.2 %all-to-all-done = f32[64,1,2048]{2,1,0:T(1,128)S(1)} async-done(((f32[64,1,2048]{2,1,0:T(1,128)}), f32[64,1,2048]{2,1,0:T(1,128)S(1)}, u32[]{:S(2)}, u32[]{:S(2)}) %all-to-all-start) | async-done | bytes 524320 | tf_op jit(solution)/shard_map/all_to_all | solution.py:77
  522.5 0.5 broadcast.100
  523.0 1.9 reduce
  524.9 0.7 reshape.77
  525.5 0.9 fusion.13
  526.5 0.1 squeeze.81
  526.8 1.0 copy.17
  527.8 0.1 squeeze.82
  527.9 1.0 copy.18
  530.6 0.6 fusion.3
  531.2 65.2 %all-reduce.2 = f32[8,2,256]{2,1,0:T(2,128)S(1)} all-reduce(f32[8,2,256]{2,1,0:T(2,128)S(1)} %copy.25), channel_id=3, replica_groups=mesh['tile'=64,'agent'=8] {'agent'}, use_global_device_ids=true, to_apply=%region_1.0.clone | all-reduce | flops 4096 | bytes 32768
  596.4 0.7 dynamic-slice_multiply_fusion
  597.1 1.9 collective-permute-start
  599.0 11.1 %collective-permute-start.1 = (f32[1,1,256]{2,1,0:T(1,128)S(1)}, f32[1,1,256]{2,1,0:T(1,128)S(1)}, u32[]{:S(2)}, u32[]{:S(2)}) collective-permute-start(f32[1,1,256]{2,1,0:T(1,128)S(1)} %get-tuple-element.27), channel_id=1, source_target_pairs={{8,0},{16,8},{24,16},{32,24},{40,32},{48,40},{56,48},{64,56},{72,6... | collective-permute-start | bytes 3080 | tf_op jit(solution)/shard_map/ppermute | solution.py:20
  610.2 1.3 collective-permute-done.1
  611.4 15.0 %collective-permute-start.2 = (f32[1,4,256]{2,1,0:T(4,128)S(1)}, f32[1,4,256]{2,1,0:T(4,128)S(1)}, u32[]{:S(2)}, u32[]{:S(2)}) collective-permute-start(f32[1,4,256]{2,1,0:T(4,128)S(1)} %pad_maximum_fusion), channel_id=1, source_target_pairs={{0,1},{1,2},{2,3},{3,4},{4,5},{5,6},{6,7},{8,9},{9,10},{10,11},{11... | collective-permute-start | bytes 12296 | tf_op jit(solution)/shard_map/ppermute | solution.py:19
  626.5 1.9 collective-permute-start.3
  628.4 14.4 %collective-permute-done.3 = f32[1,4,256]{2,1,0:T(4,128)S(1)} collective-permute-done((f32[1,4,256]{2,1,0:T(4,128)S(1)}, f32[1,4,256]{2,1,0:T(4,128)S(1)}, u32[]{:S(2)}, u32[]{:S(2)}) %collective-permute-start.3) | collective-permute-done | bytes 4128 | tf_op jit(solution)/shard_map/ppermute | solution.py:20
  642.9 0.2 add_divide_fusion.1
  643.1 1.9 collective-permute-start.4
  645.0 11.1 %collective-permute-start.5 = (f32[1,1,256]{2,1,0:T(1,128)S(1)}, f32[1,1,256]{2,1,0:T(1,128)S(1)}, u32[]{:S(2)}, u32[]{:S(2)}) collective-permute-start(f32[1,1,256]{2,1,0:T(1,128)S(1)} %get-tuple-element.25), channel_id=1, source_target_pairs={{8,0},{16,8},{24,16},{32,24},{40,32},{48,40},{56,48},{64,56},{72,6... | collective-permute-start | bytes 3080 | tf_op jit(solution)/shard_map/ppermute | solution.py:20
  656.2 1.3 collective-permute-done.5
  657.5 1.9 collective-permute-start.6
  659.4 3.9 collective-permute-start.7
  663.3 12.4 %collective-permute-done.7 = f32[1,4,256]{2,1,0:T(4,128)S(1)} collective-permute-done((f32[1,4,256]{2,1,0:T(4,128)S(1)}, f32[1,4,256]{2,1,0:T(4,128)S(1)}, u32[]{:S(2)}, u32[]{:S(2)}) %collective-permute-start.7) | collective-permute-done | bytes 4128 | tf_op jit(solution)/shard_map/ppermute | solution.py:20
  675.8 0.9 add_divide_fusion
  676.7 57.1 %all_gather.3 = f32[8,2,256]{2,1,0:T(2,128)S(1)} all-gather(f32[1,2,256]{2,1,0:T(2,128)S(1)} %add_divide_fusion), channel_id=1, replica_groups=mesh['tile'=64,'agent'=8] {'agent'}, dimensions={0}, use_global_device_ids=true | all-gather | bytes 18432 | tf_op jit(solution)/shard_map/all_gather | solution.py:97
  733.8 0.6 copy.27
  734.4 0.6 copy.68
  (61 shorter events, 2.3 us)
Async XLA Ops:
  7.2 439.6 %reduce-scatter.4.cloned.1.call-start = ((), (), s32[]{:S(2)}) async-start(), calls=%async_computation.2 | async-start | bytes 1064960
  34.4 413.3 %copy-start.2 = (f32[8,8,32]{2,1,0:T(8,128)S(1)}, f32[8,8,32]{2,1,0:T(8,128)}, u32[]{:S(2)}) copy-start(f32[8,8,32]{2,1,0:T(8,128)} %param.9) | copy-start | bytes 24580
  34.4 413.3 %copy-start.3 = (f32[8,8,32]{2,1,0:T(8,128)S(1)}, f32[8,8,32]{2,1,0:T(8,128)}, u32[]{:S(2)}) copy-start(f32[8,8,32]{2,1,0:T(8,128)} %param.8) | copy-start | bytes 24580
  449.6 72.8 %all-to-all-start = ((f32[64,1,2048]{2,1,0:T(1,128)}), f32[64,1,2048]{2,1,0:T(1,128)S(1)}, u32[]{:S(2)}, u32[]{:S(2)}) async-start(f32[64,1,2048]{2,1,0:T(1,128)} %reshape.76), calls=%async_computation | async-start | bytes 1048576 | tf_op jit(solution)/shard_map/all_to_all | solution.py:77
  529.1 1.5 copy-start
  529.1 1.5 copy-start.1
  597.1 13.1 %collective-permute-start = (f32[1,1,256]{2,1,0:T(1,128)S(1)}, f32[1,1,256]{2,1,0:T(1,128)S(1)}, u32[]{:S(2)}, u32[]{:S(2)}) collective-permute-start(f32[1,1,256]{2,1,0:T(1,128)S(1)} %get-tuple-element.26), channel_id=1, source_target_pairs={{0,8},{8,16},{16,24},{24,32},{32,40},{40,48},{48,56},{56,64},{64,7... | collective-permute-start | bytes 3080 | tf_op jit(solution)/shard_map/ppermute | solution.py:19
  599.0 12.4 %collective-permute-start.1 = (f32[1,1,256]{2,1,0:T(1,128)S(1)}, f32[1,1,256]{2,1,0:T(1,128)S(1)}, u32[]{:S(2)}, u32[]{:S(2)}) collective-permute-start(f32[1,1,256]{2,1,0:T(1,128)S(1)} %get-tuple-element.27), channel_id=1, source_target_pairs={{8,0},{16,8},{24,16},{32,24},{40,32},{48,40},{56,48},{64,56},{72,6... | collective-permute-start | bytes 3080 | tf_op jit(solution)/shard_map/ppermute | solution.py:20
  611.4 16.9 %collective-permute-start.2 = (f32[1,4,256]{2,1,0:T(4,128)S(1)}, f32[1,4,256]{2,1,0:T(4,128)S(1)}, u32[]{:S(2)}, u32[]{:S(2)}) collective-permute-start(f32[1,4,256]{2,1,0:T(4,128)S(1)} %pad_maximum_fusion), channel_id=1, source_target_pairs={{0,1},{1,2},{2,3},{3,4},{4,5},{5,6},{6,7},{8,9},{9,10},{10,11},{11... | collective-permute-start | bytes 12296 | tf_op jit(solution)/shard_map/ppermute | solution.py:19
  626.5 16.3 %collective-permute-start.3 = (f32[1,4,256]{2,1,0:T(4,128)S(1)}, f32[1,4,256]{2,1,0:T(4,128)S(1)}, u32[]{:S(2)}, u32[]{:S(2)}) collective-permute-start(f32[1,4,256]{2,1,0:T(4,128)S(1)} %pad_maximum_fusion), channel_id=1, source_target_pairs={{1,0},{2,1},{3,2},{4,3},{5,4},{6,5},{7,6},{9,8},{10,9},{11,10},{12... | collective-permute-start | bytes 12296 | tf_op jit(solution)/shard_map/ppermute | solution.py:20
  643.1 13.1 %collective-permute-start.4 = (f32[1,1,256]{2,1,0:T(1,128)S(1)}, f32[1,1,256]{2,1,0:T(1,128)S(1)}, u32[]{:S(2)}, u32[]{:S(2)}) collective-permute-start(f32[1,1,256]{2,1,0:T(1,128)S(1)} %get-tuple-element.24), channel_id=1, source_target_pairs={{0,8},{8,16},{16,24},{24,32},{32,40},{40,48},{48,56},{56,64},{64,7... | collective-permute-start | bytes 3080 | tf_op jit(solution)/shard_map/ppermute | solution.py:19
  645.0 12.4 %collective-permute-start.5 = (f32[1,1,256]{2,1,0:T(1,128)S(1)}, f32[1,1,256]{2,1,0:T(1,128)S(1)}, u32[]{:S(2)}, u32[]{:S(2)}) collective-permute-start(f32[1,1,256]{2,1,0:T(1,128)S(1)} %get-tuple-element.25), channel_id=1, source_target_pairs={{8,0},{16,8},{24,16},{32,24},{40,32},{48,40},{56,48},{64,56},{72,6... | collective-permute-start | bytes 3080 | tf_op jit(solution)/shard_map/ppermute | solution.py:20
  657.5 5.8 collective-permute-start.6
  659.4 16.3 %collective-permute-start.7 = (f32[1,4,256]{2,1,0:T(4,128)S(1)}, f32[1,4,256]{2,1,0:T(4,128)S(1)}, u32[]{:S(2)}, u32[]{:S(2)}) collective-permute-start(f32[1,4,256]{2,1,0:T(4,128)S(1)} %pad_maximum_fusion.1), channel_id=1, source_target_pairs={{1,0},{2,1},{3,2},{4,3},{5,4},{6,5},{7,6},{9,8},{10,9},{11,10},{12... | collective-permute-start | bytes 12296 | tf_op jit(solution)/shard_map/ppermute | solution.py:20
Sparse Core Ops, SparseCore 0:
  41.0 405.6 reduce-scatter.3
